TPU v7x, 32 devices: a whole 2x2x4 slice. The times are simulated.
32 devices in a mesh: outer: 2 (over x), inner: 16 (over z, y, core).
Axes of the slice: x: 2, y: 2, z: 4, core: 2. Of those that a mesh axis runs over, the one named last changes fastest.
Arguments:
- points: bfloat16 [16, 131072], P(None, ('outer', 'inner')), may hold values from -3 to 3
- charges: bfloat16 [64, 131072], P(None, ('outer', 'inner')), may hold values from -6 to 6
- near_leaves: int32 [512, 16], P(('outer', 'inner')), may hold values from 0 to 511, as said below
- skel_device: int32 [32, 512], P(('outer', 'inner')), may hold values from 0 to 4095, as said below
- skel_tree: int32 [32, 4, 512], P(('outer', 'inner')), may hold values from 0 to 1023, as said below
Outputs:
- potential: float32 [64, 131072], P(None, ('outer', 'inner'))
Inputs may be any that keep to these rules, and one draw needn't show every extreme that they name: `near_leaves`: row b holds 16 different leaf numbers, b among them, each a leaf of b's level-0 node or of the level-0 nodes just before and just after it. `skel_device`: row c holds 512 different offsets among the 4096 points of level-0 node c. skel_tree[c, k] holds 512 different positions among the 1024 skeleton points of the children of the level-(k+1) node that contains level-0 node c; all level-0 nodes inside one level-(k+1) node have equal rows k.
All inputs are finite; a program needn't handle non-finite values.
Results may differ from a plain program's by a relative error of at most 0.0035.
Values may be sent and summed in bfloat16 or wider, within the bound.
A program may use at most 64 MiB of HBM per device.

v0:
```python
import jax
import jax.numpy as jnp
from jax import lax
from jax.sharding import PartitionSpec as P

DIM = 16
NRHS = 64


GAMMA = 0.125


def partner(block, axis, stride):
    count = lax.axis_size(axis)
    route = []
    for low in range(count):
        high = low | 1 << stride
        if high != low and high < count:
            route += [(low, high), (high, low)]
    return lax.ppermute(block, axis, route)


def extended_2(array, sides, width):
    for axis, dim in sides:
        peers, length = (lax.axis_size(axis), array.shape[dim])
        up = [(i, (i + 1) % peers) for i in range(peers - 1)]
        down = [(j, i) for i, j in up]
        last = lax.slice_in_dim(array, length - width, length, axis=dim)
        leading = lax.slice_in_dim(array, 0, width, axis=dim)
        before = lax.ppermute(last, axis, up)
        after = lax.ppermute(leading, axis, down)
        array = jnp.concatenate([before, array, after], axis=dim)
    return array


def kernel_block(left, right):
    left32 = left.astype(jnp.float32)
    right32 = right.astype(jnp.float32)
    products = jnp.einsum("dm,dn->mn", left, right, preferred_element_type=jnp.float32)
    distance = (
        jnp.sum(left32 * left32, 0)[:, None]
        + jnp.sum(right32 * right32, 0)[None, :]
        - 2.0 * products
    )
    return jnp.exp(-GAMMA * distance).astype(jnp.bfloat16)


def spread_weights(weights, block):
    totals = jnp.sum(block.astype(jnp.float32), 1)
    return (weights.astype(jnp.float32) / totals[None, :]).astype(jnp.bfloat16)


def carry_values(values, block):
    totals = jnp.sum(block.astype(jnp.float32), 0)
    return jnp.dot(values, block, preferred_element_type=jnp.float32) / totals[None, :]


def parent_node(joined, chosen):
    joined_x = joined[:DIM]
    parent_x = jnp.take(joined_x, chosen, axis=1)
    block = kernel_block(joined_x, parent_x)
    parent_up = jnp.dot(
        spread_weights(joined[DIM:], block), block, preferred_element_type=jnp.float32
    ).astype(jnp.bfloat16)
    return jnp.concatenate([parent_x, parent_up], 0)


def downward_top(sibling, own_x):
    return jnp.dot(
        sibling[DIM:], kernel_block(sibling[:DIM], own_x), preferred_element_type=jnp.float32
    ).astype(jnp.bfloat16)


def downward_node(sibling, parent_x, parent_down, own_x):
    beside = jnp.dot(
        sibling[DIM:], kernel_block(sibling[:DIM], own_x), preferred_element_type=jnp.float32
    )
    above = carry_values(parent_down, kernel_block(parent_x, own_x))
    return (beside + above).astype(jnp.bfloat16)


def near_block(leaves, targets_x, leaf_ids):
    target32 = targets_x.astype(jnp.float32)
    target_norm = jnp.sum(target32 * target32, 1)

    def one_turn(turn, summed):
        source = jnp.take(leaves, leaf_ids[:, turn], axis=0)
        source_x = source[:, :DIM]
        source32 = source_x.astype(jnp.float32)
        products = jnp.einsum(
            "bdt,bds->bts", targets_x, source_x, preferred_element_type=jnp.float32
        )
        distance = (
            target_norm[:, :, None] + jnp.sum(source32 * source32, 1)[:, None, :] - 2.0 * products
        )
        weights = jnp.exp(-GAMMA * distance).astype(jnp.bfloat16)
        return summed + jnp.einsum(
            "bts,brs->rbt", weights, source[:, DIM:], preferred_element_type=jnp.float32
        )

    start = jnp.zeros((NRHS, targets_x.shape[0], targets_x.shape[2]), jnp.float32)
    return lax.fori_loop(0, leaf_ids.shape[1], one_turn, start)


def swap_inner(node_data, bit_index):
    return partner(node_data, "inner", bit_index)


def swap_outer(node_data, bit_index):
    return partner(node_data, "outer", bit_index)


def climb_swap(node_data, skel_rows, records, parents, first, number, exchange, position, levels):
    for offset in range(number):
        height = first + offset
        sibling = exchange(node_data, offset)
        records.append((node_data[:DIM], sibling))
        if height < levels - 1:
            is_right = position >> offset & 1 == 1
            joined = jnp.where(
                is_right,
                jnp.concatenate([sibling, node_data], 1),
                jnp.concatenate([node_data, sibling], 1),
            )
            node_data = parent_node(joined, skel_rows[height])
            parents.append(node_data[:DIM])
    return node_data


def body(points, charges, near_leaves, skel_device, skel_tree):
    inner_levels = lax.axis_size("inner").bit_length() - 1
    outer_levels = lax.axis_size("outer").bit_length() - 1
    levels = inner_levels + outer_levels
    position = lax.axis_index(("outer", "inner"))
    dev_points = points.shape[1]
    leaf_dev = near_leaves.shape[0]
    leaf_size = dev_points // leaf_dev
    stacked = jnp.concatenate([points, charges], 0)
    extended = extended_2(stacked, ((("outer", "inner"), 1),), dev_points)
    base_x = jnp.take(points, skel_device[0], axis=1)
    base_block = kernel_block(points, base_x)
    base_up = jnp.dot(
        spread_weights(charges, base_block), base_block, preferred_element_type=jnp.float32
    ).astype(jnp.bfloat16)
    node_data = jnp.concatenate([base_x, base_up], 0)
    skel_rows = skel_tree[0]
    records = []
    parents = []
    node_data = climb_swap(
        node_data,
        skel_rows,
        records,
        parents,
        0,
        inner_levels,
        swap_inner,
        lax.axis_index("inner"),
        levels,
    )
    node_data = climb_swap(
        node_data,
        skel_rows,
        records,
        parents,
        inner_levels,
        outer_levels,
        swap_outer,
        lax.axis_index("outer"),
        levels,
    )
    downward = None
    for height in range(levels - 1, -1, -1):
        own_x, sibling = records[height]
        if height == levels - 1:
            downward = downward_top(sibling, own_x)
        else:
            downward = downward_node(sibling, parents[height], downward, own_x)
    far_part = carry_values(downward, kernel_block(base_x, points))
    leaves = extended.reshape(DIM + NRHS, 3 * leaf_dev, leaf_size).transpose(1, 0, 2)
    targets_x = points.reshape(DIM, leaf_dev, leaf_size).transpose(1, 0, 2)
    leaf_ids = near_leaves - (position - 1) * leaf_dev
    near_part = near_block(leaves, targets_x, leaf_ids)
    return near_part.reshape(NRHS, dev_points) + far_part


def solution(mesh):
    return jax.shard_map(
        body,
        mesh=mesh,
        in_specs=(
            P(None, ("outer", "inner")),
            P(None, ("outer", "inner")),
            P(("outer", "inner"), None),
            P(("outer", "inner"), None),
            P(("outer", "inner"), None, None),
        ),
        out_specs=P(None, ("outer", "inner")),
        check_vma=False,
    )
```

profile of v0, /device:TPU:0, one launch (start us, length us, event | category | flops | bytes accessed | tf_op | source)
XLA Modules:
  0.0 153.8 jit_solution(2646203638078710570)
XLA Ops:
  0.0 1.0 constant_dynamic-update-slice_fusion.1
  1.0 1.1 constant_dynamic-update-slice_fusion
  2.1 2.4 %collective-permute-start = (bf16[80,4096]{1,0:T(8,128)(2,1)S(1)}, bf16[80,4096]{1,0:T(8,128)(2,1)S(1)}, u32[]{:S(2)}, u32[]{:S(2)}) collective-permute-start(bf16[80,4096]{1,0:T(8,128)(2,1)S(1)} %constant_dynamic-update-slice_fusion), channel_id=1, source_target_pairs={{0,1},{1,2},{2,3},{3,4},{4,5},{5,6},{6,7},{7,8},{8,9},{9,10},{10,1... | collective-permute-start | bytes 1966088 | tf_op jit(solution)/shard_map/ppermute | solution.py:30
  4.5 1.3 collective-permute-start.1
  5.8 1.4 copy.22
  7.3 1.3 gather_fusion.1
  8.8 4.6 %convert_reduce_fusion.1 = (f32[4096]{0:T(1024)S(1)}, bf16[4096,512]{0,1:T(8,128)(2,1)S(1)}, f32[512,4096]{1,0:T(8,128)}) fusion(f32[512]{0:T(512)S(1)} %get-tuple-element.169, f32[4096]{0:T(1024)S(1)} %multiply_reduce_fusion.1, bf16[16,4096]{1,0:T(8,128)(2,1)S(1)} %copy-done, bf16[512,16]{0,1:T(8,128)(2,1)S(1)} %copy.23, ...), kind=kOutput, calls=%fused_computation.28 | convolution fusion | flops 81793024 | bytes 12765696 | tf_op jit(solution)/shard_map/dm,dn->mn/dot_general | solution.py:39
  13.4 1.4 convolution_convert_fusion.4
  14.8 3.3 %collective-permute-start.2 = (bf16[80,512]{1,0:T(8,128)(2,1)S(1)}, bf16[80,512]{1,0:T(8,128)(2,1)S(1)}, u32[]{:S(2)}, u32[]{:S(2)}) collective-permute-start(bf16[80,512]{1,0:T(8,128)(2,1)S(1)} %pad_maximum_fusion.1), channel_id=1, source_target_pairs={{0,1},{1,0},{2,3},{3,2},{4,5},{5,4},{6,7},{7,6},{8,9},{9,8},{10,11... | collective-permute-start | bytes 245768 | tf_op jit(solution)/shard_map/ppermute | solution.py:20
  18.2 5.9 %convert_reduce_fusion = (f32[4096]{0:T(1024)S(1)}, bf16[512,4096]{1,0:T(8,128)(2,1)}) fusion(f32[512,4096]{1,0:T(8,128)} %get-tuple-element.175, f32[4096]{0:T(1024)S(1)} %multiply_reduce_fusion.1, f32[512]{0:T(512)S(1)} %get-tuple-element.169), kind=kLoop, calls=%fused_computation.26 | loop fusion | flops 14675968 | bytes 12617728 | tf_op jit(solution)/shard_map/reduce_sum | solution.py:54
  24.6 1.3 gather_fusion.2
  26.1 1.2 convert_reduce_fusion.6
  27.3 0.7 convert_reduce_fusion.5
  28.5 1.7 %collective-permute-start.3 = (bf16[80,512]{1,0:T(8,128)(2,1)S(1)}, bf16[80,512]{1,0:T(8,128)(2,1)S(1)}, u32[]{:S(2)}, u32[]{:S(2)}) collective-permute-start(bf16[80,512]{1,0:T(8,128)(2,1)S(1)} %pad_maximum_fusion.2), channel_id=1, source_target_pairs={{0,2},{2,0},{1,3},{3,1},{4,6},{6,4},{5,7},{7,5},{8,10},{10,8},{9,1... | collective-permute-start | bytes 245768 | tf_op jit(solution)/shard_map/ppermute | solution.py:20
  30.3 3.1 %collective-permute-done.3 = bf16[80,512]{1,0:T(8,128)(2,1)S(1)} collective-permute-done((bf16[80,512]{1,0:T(8,128)(2,1)S(1)}, bf16[80,512]{1,0:T(8,128)(2,1)S(1)}, u32[]{:S(2)}, u32[]{:S(2)}) %collective-permute-start.3) | collective-permute-done | bytes 81952 | tf_op jit(solution)/shard_map/ppermute | solution.py:20
  33.6 1.3 gather_fusion.3
  35.1 1.3 convert_reduce_fusion.7
  36.3 0.7 convert_reduce_fusion.4
  37.5 2.8 %collective-permute-start.4 = (bf16[80,512]{1,0:T(8,128)(2,1)S(1)}, bf16[80,512]{1,0:T(8,128)(2,1)S(1)}, u32[]{:S(2)}, u32[]{:S(2)}) collective-permute-start(bf16[80,512]{1,0:T(8,128)(2,1)S(1)} %pad_maximum_fusion.3), channel_id=1, source_target_pairs={{0,4},{4,0},{1,5},{5,1},{2,6},{6,2},{3,7},{7,3},{8,12},{12,8},{9,1... | collective-permute-start | bytes 245768 | tf_op jit(solution)/shard_map/ppermute | solution.py:20
  40.3 2.4 %collective-permute-done.4 = bf16[80,512]{1,0:T(8,128)(2,1)S(1)} collective-permute-done((bf16[80,512]{1,0:T(8,128)(2,1)S(1)}, bf16[80,512]{1,0:T(8,128)(2,1)S(1)}, u32[]{:S(2)}, u32[]{:S(2)}) %collective-permute-start.4) | collective-permute-done | bytes 81952 | tf_op jit(solution)/shard_map/ppermute | solution.py:20
  43.0 1.3 gather_fusion.4
  44.4 1.3 convert_reduce_fusion.8
  45.7 0.7 convert_reduce_fusion.3
  46.9 3.1 %collective-permute-start.5 = (bf16[80,512]{1,0:T(8,128)(2,1)S(1)}, bf16[80,512]{1,0:T(8,128)(2,1)S(1)}, u32[]{:S(2)}, u32[]{:S(2)}) collective-permute-start(bf16[80,512]{1,0:T(8,128)(2,1)S(1)} %pad_maximum_fusion.4), channel_id=1, source_target_pairs={{0,8},{8,0},{1,9},{9,1},{2,10},{10,2},{3,11},{11,3},{4,12},{12,4},... | collective-permute-start | bytes 245768 | tf_op jit(solution)/shard_map/ppermute | solution.py:20
  50.0 2.4 %collective-permute-done.5 = bf16[80,512]{1,0:T(8,128)(2,1)S(1)} collective-permute-done((bf16[80,512]{1,0:T(8,128)(2,1)S(1)}, bf16[80,512]{1,0:T(8,128)(2,1)S(1)}, u32[]{:S(2)}, u32[]{:S(2)}) %collective-permute-start.5) | collective-permute-done | bytes 81952 | tf_op jit(solution)/shard_map/ppermute | solution.py:20
  52.7 1.5 gather_fusion.5
  54.8 0.7 convert_reduce_fusion.2
  56.0 4.9 %collective-permute-start.6 = (bf16[80,512]{1,0:T(8,128)(2,1)S(1)}, bf16[80,512]{1,0:T(8,128)(2,1)S(1)}, u32[]{:S(2)}, u32[]{:S(2)}) collective-permute-start(bf16[80,512]{1,0:T(8,128)(2,1)S(1)} %pad_maximum_fusion.5), channel_id=1, source_target_pairs={{0,16},{16,0},{1,17},{17,1},{2,18},{18,2},{3,19},{19,3},{4,20},{20... | collective-permute-start | bytes 245768 | tf_op jit(solution)/shard_map/ppermute | solution.py:20
  60.9 2.4 %collective-permute-done.6 = bf16[80,512]{1,0:T(8,128)(2,1)S(1)} collective-permute-done((bf16[80,512]{1,0:T(8,128)(2,1)S(1)}, bf16[80,512]{1,0:T(8,128)(2,1)S(1)}, u32[]{:S(2)}, u32[]{:S(2)}) %collective-permute-start.6) | collective-permute-done | bytes 81952 | tf_op jit(solution)/shard_map/ppermute | solution.py:20
  64.7 1.9 %convolution_divide_fusion.3 = f32[64,512]{1,0:T(8,128)} fusion(bf16[64,512]{1,0:T(8,128)(2,1)S(1)} %fusion.60, bf16[512,512]{1,0:T(8,128)(2,1)} %get-tuple-element.187, f32[512]{0:T(512)S(1)} %get-tuple-element.186), kind=kOutput, calls=%fused_computation.92 | convolution fusion | flops 33587200 | bytes 722944 | tf_op jit(solution)/shard_map/dot_general | solution.py:55
  66.6 2.1 %fusion.61 = bf16[64,512]{1,0:T(8,128)(2,1)} fusion(f32[64,512]{1,0:T(8,128)} %convolution_divide_fusion.3, bf16[16,512]{1,0:T(8,128)(2,1)S(1)} %get-tuple-element.164, f32[512]{0:T(512)S(1)} %get-tuple-element.163, f32[512]{0:T(512)S(1)} %multiply_reduce_fusion.11, bf16[80,512]{1,0:T(8,128)(2,1)S(1)} %collective-permute-done.4), kind=kOutput, calls=%fused_computation.103 | convolution fusion | flops 43319296 | bytes 299008 | tf_op jit(solution)/shard_map/dot_general | solution.py:75
  68.8 1.7 %convolution_divide_fusion.2 = f32[64,512]{1,0:T(8,128)} fusion(bf16[64,512]{1,0:T(8,128)(2,1)} %fusion.61, bf16[512,512]{1,0:T(8,128)(2,1)S(1)} %copy-done.6, f32[512]{0:T(512)S(1)} %get-tuple-element.188), kind=kOutput, calls=%fused_computation.91 | convolution fusion | flops 33587200 | bytes 722944 | tf_op jit(solution)/shard_map/dot_general | solution.py:55
  70.5 1.5 fusion.62
  72.1 1.2 fusion.63
  73.9 0.7 copy.19
  74.6 73.8 %while.14 = (s32[]{:T(128)}, f32[64,16,256]{2,0,1:T(8,128)}, s32[16,16]{0,1:T(8,128)S(1)}, bf16[48,80,256]{2,1,0:T(8,128)(2,1)S(1)}, f32[16,256]{1,0:T(8,128)S(1...) while((s32[]{:T(128)}, f32[64,16,256]{2,0,1:T(8,128)}, s32[16,16]{0,1:T(8,128)S(1)}, ...), condition=%wide.region_3.4_spmd.clone, body=%wide.region_1.3_spmd.clone.sunk | while | flops 174060640 | bytes 5689731 | solution.py:102
  74.6 0.6 gather_fusion
  75.4 2.6 %fusion.180 = f32[64,16,256]{2,0,1:T(8,128)} fusion(bf16[16,16,256]{2,1,0:T(8,128)(2,1)S(1)} %get-tuple-element.258, f32[16,256]{1,0:T(8,128)S(1)} %multiply_reduce_fusion.18, f32[16,256]{1,0:T(8,128)S(1)} %get-tuple-element.257, f32[64,16,256]{2,0,1:T(8,128)} %get-tuple-element.246, bf16[16,80,256]{2,1,0:T(8,128)(2,1)S(1)} %broadcast_select_fusion.7, ...), kind=kOutput, calls=%fused_computation.12.clone.1 | convolution fusion | flops 173539328 | bytes 2916353 | tf_op jit(solution)/shard_map/while/body/eval_jaxpr/bts,brs->rbt/dot_general | solution.py:97
  78.1 0.6 gather_fusion
  78.9 3.9 %fusion.180 = f32[64,16,256]{2,0,1:T(8,128)} fusion(bf16[16,16,256]{2,1,0:T(8,128)(2,1)S(1)} %get-tuple-element.258, f32[16,256]{1,0:T(8,128)S(1)} %multiply_reduce_fusion.18, f32[16,256]{1,0:T(8,128)S(1)} %get-tuple-element.257, f32[64,16,256]{2,0,1:T(8,128)} %get-tuple-element.246, bf16[16,80,256]{2,1,0:T(8,128)(2,1)S(1)} %broadcast_select_fusion.7, ...), kind=kOutput, calls=%fused_computation.12.clone.1 | convolution fusion | flops 173539328 | bytes 2916353 | tf_op jit(solution)/shard_map/while/body/eval_jaxpr/bts,brs->rbt/dot_general | solution.py:97
  82.8 0.6 gather_fusion
  83.6 3.9 %fusion.180 = f32[64,16,256]{2,0,1:T(8,128)} fusion(bf16[16,16,256]{2,1,0:T(8,128)(2,1)S(1)} %get-tuple-element.258, f32[16,256]{1,0:T(8,128)S(1)} %multiply_reduce_fusion.18, f32[16,256]{1,0:T(8,128)S(1)} %get-tuple-element.257, f32[64,16,256]{2,0,1:T(8,128)} %get-tuple-element.246, bf16[16,80,256]{2,1,0:T(8,128)(2,1)S(1)} %broadcast_select_fusion.7, ...), kind=kOutput, calls=%fused_computation.12.clone.1 | convolution fusion | flops 173539328 | bytes 2916353 | tf_op jit(solution)/shard_map/while/body/eval_jaxpr/bts,brs->rbt/dot_general | solution.py:97
  87.5 0.6 gather_fusion
  88.3 3.9 %fusion.180 = f32[64,16,256]{2,0,1:T(8,128)} fusion(bf16[16,16,256]{2,1,0:T(8,128)(2,1)S(1)} %get-tuple-element.258, f32[16,256]{1,0:T(8,128)S(1)} %multiply_reduce_fusion.18, f32[16,256]{1,0:T(8,128)S(1)} %get-tuple-element.257, f32[64,16,256]{2,0,1:T(8,128)} %get-tuple-element.246, bf16[16,80,256]{2,1,0:T(8,128)(2,1)S(1)} %broadcast_select_fusion.7, ...), kind=kOutput, calls=%fused_computation.12.clone.1 | convolution fusion | flops 173539328 | bytes 2916353 | tf_op jit(solution)/shard_map/while/body/eval_jaxpr/bts,brs->rbt/dot_general | solution.py:97
  92.2 0.6 gather_fusion
  93.0 3.9 %fusion.180 = f32[64,16,256]{2,0,1:T(8,128)} fusion(bf16[16,16,256]{2,1,0:T(8,128)(2,1)S(1)} %get-tuple-element.258, f32[16,256]{1,0:T(8,128)S(1)} %multiply_reduce_fusion.18, f32[16,256]{1,0:T(8,128)S(1)} %get-tuple-element.257, f32[64,16,256]{2,0,1:T(8,128)} %get-tuple-element.246, bf16[16,80,256]{2,1,0:T(8,128)(2,1)S(1)} %broadcast_select_fusion.7, ...), kind=kOutput, calls=%fused_computation.12.clone.1 | convolution fusion | flops 173539328 | bytes 2916353 | tf_op jit(solution)/shard_map/while/body/eval_jaxpr/bts,brs->rbt/dot_general | solution.py:97
  97.6 3.9 %fusion.180 = f32[64,16,256]{2,0,1:T(8,128)} fusion(bf16[16,16,256]{2,1,0:T(8,128)(2,1)S(1)} %get-tuple-element.258, f32[16,256]{1,0:T(8,128)S(1)} %multiply_reduce_fusion.18, f32[16,256]{1,0:T(8,128)S(1)} %get-tuple-element.257, f32[64,16,256]{2,0,1:T(8,128)} %get-tuple-element.246, bf16[16,80,256]{2,1,0:T(8,128)(2,1)S(1)} %broadcast_select_fusion.7, ...), kind=kOutput, calls=%fused_computation.12.clone.1 | convolution fusion | flops 173539328 | bytes 2916353 | tf_op jit(solution)/shard_map/while/body/eval_jaxpr/bts,brs->rbt/dot_general | solution.py:97
  101.5 0.6 gather_fusion
  102.3 3.9 %fusion.180 = f32[64,16,256]{2,0,1:T(8,128)} fusion(bf16[16,16,256]{2,1,0:T(8,128)(2,1)S(1)} %get-tuple-element.258, f32[16,256]{1,0:T(8,128)S(1)} %multiply_reduce_fusion.18, f32[16,256]{1,0:T(8,128)S(1)} %get-tuple-element.257, f32[64,16,256]{2,0,1:T(8,128)} %get-tuple-element.246, bf16[16,80,256]{2,1,0:T(8,128)(2,1)S(1)} %broadcast_select_fusion.7, ...), kind=kOutput, calls=%fused_computation.12.clone.1 | convolution fusion | flops 173539328 | bytes 2916353 | tf_op jit(solution)/shard_map/while/body/eval_jaxpr/bts,brs->rbt/dot_general | solution.py:97
  107.0 3.9 %fusion.180 = f32[64,16,256]{2,0,1:T(8,128)} fusion(bf16[16,16,256]{2,1,0:T(8,128)(2,1)S(1)} %get-tuple-element.258, f32[16,256]{1,0:T(8,128)S(1)} %multiply_reduce_fusion.18, f32[16,256]{1,0:T(8,128)S(1)} %get-tuple-element.257, f32[64,16,256]{2,0,1:T(8,128)} %get-tuple-element.246, bf16[16,80,256]{2,1,0:T(8,128)(2,1)S(1)} %broadcast_select_fusion.7, ...), kind=kOutput, calls=%fused_computation.12.clone.1 | convolution fusion | flops 173539328 | bytes 2916353 | tf_op jit(solution)/shard_map/while/body/eval_jaxpr/bts,brs->rbt/dot_general | solution.py:97
  110.9 0.6 gather_fusion
  111.7 3.9 %fusion.180 = f32[64,16,256]{2,0,1:T(8,128)} fusion(bf16[16,16,256]{2,1,0:T(8,128)(2,1)S(1)} %get-tuple-element.258, f32[16,256]{1,0:T(8,128)S(1)} %multiply_reduce_fusion.18, f32[16,256]{1,0:T(8,128)S(1)} %get-tuple-element.257, f32[64,16,256]{2,0,1:T(8,128)} %get-tuple-element.246, bf16[16,80,256]{2,1,0:T(8,128)(2,1)S(1)} %broadcast_select_fusion.7, ...), kind=kOutput, calls=%fused_computation.12.clone.1 | convolution fusion | flops 173539328 | bytes 2916353 | tf_op jit(solution)/shard_map/while/body/eval_jaxpr/bts,brs->rbt/dot_general | solution.py:97
  116.4 3.9 %fusion.180 = f32[64,16,256]{2,0,1:T(8,128)} fusion(bf16[16,16,256]{2,1,0:T(8,128)(2,1)S(1)} %get-tuple-element.258, f32[16,256]{1,0:T(8,128)S(1)} %multiply_reduce_fusion.18, f32[16,256]{1,0:T(8,128)S(1)} %get-tuple-element.257, f32[64,16,256]{2,0,1:T(8,128)} %get-tuple-element.246, bf16[16,80,256]{2,1,0:T(8,128)(2,1)S(1)} %broadcast_select_fusion.7, ...), kind=kOutput, calls=%fused_computation.12.clone.1 | convolution fusion | flops 173539328 | bytes 2916353 | tf_op jit(solution)/shard_map/while/body/eval_jaxpr/bts,brs->rbt/dot_general | solution.py:97
  121.1 3.9 %fusion.180 = f32[64,16,256]{2,0,1:T(8,128)} fusion(bf16[16,16,256]{2,1,0:T(8,128)(2,1)S(1)} %get-tuple-element.258, f32[16,256]{1,0:T(8,128)S(1)} %multiply_reduce_fusion.18, f32[16,256]{1,0:T(8,128)S(1)} %get-tuple-element.257, f32[64,16,256]{2,0,1:T(8,128)} %get-tuple-element.246, bf16[16,80,256]{2,1,0:T(8,128)(2,1)S(1)} %broadcast_select_fusion.7, ...), kind=kOutput, calls=%fused_computation.12.clone.1 | convolution fusion | flops 173539328 | bytes 2916353 | tf_op jit(solution)/shard_map/while/body/eval_jaxpr/bts,brs->rbt/dot_general | solution.py:97
  125.0 0.6 gather_fusion
  125.8 3.9 %fusion.180 = f32[64,16,256]{2,0,1:T(8,128)} fusion(bf16[16,16,256]{2,1,0:T(8,128)(2,1)S(1)} %get-tuple-element.258, f32[16,256]{1,0:T(8,128)S(1)} %multiply_reduce_fusion.18, f32[16,256]{1,0:T(8,128)S(1)} %get-tuple-element.257, f32[64,16,256]{2,0,1:T(8,128)} %get-tuple-element.246, bf16[16,80,256]{2,1,0:T(8,128)(2,1)S(1)} %broadcast_select_fusion.7, ...), kind=kOutput, calls=%fused_computation.12.clone.1 | convolution fusion | flops 173539328 | bytes 2916353 | tf_op jit(solution)/shard_map/while/body/eval_jaxpr/bts,brs->rbt/dot_general | solution.py:97
  130.5 3.9 %fusion.180 = f32[64,16,256]{2,0,1:T(8,128)} fusion(bf16[16,16,256]{2,1,0:T(8,128)(2,1)S(1)} %get-tuple-element.258, f32[16,256]{1,0:T(8,128)S(1)} %multiply_reduce_fusion.18, f32[16,256]{1,0:T(8,128)S(1)} %get-tuple-element.257, f32[64,16,256]{2,0,1:T(8,128)} %get-tuple-element.246, bf16[16,80,256]{2,1,0:T(8,128)(2,1)S(1)} %broadcast_select_fusion.7, ...), kind=kOutput, calls=%fused_computation.12.clone.1 | convolution fusion | flops 173539328 | bytes 2916353 | tf_op jit(solution)/shard_map/while/body/eval_jaxpr/bts,brs->rbt/dot_general | solution.py:97
  134.4 0.6 gather_fusion
  135.2 3.9 %fusion.180 = f32[64,16,256]{2,0,1:T(8,128)} fusion(bf16[16,16,256]{2,1,0:T(8,128)(2,1)S(1)} %get-tuple-element.258, f32[16,256]{1,0:T(8,128)S(1)} %multiply_reduce_fusion.18, f32[16,256]{1,0:T(8,128)S(1)} %get-tuple-element.257, f32[64,16,256]{2,0,1:T(8,128)} %get-tuple-element.246, bf16[16,80,256]{2,1,0:T(8,128)(2,1)S(1)} %broadcast_select_fusion.7, ...), kind=kOutput, calls=%fused_computation.12.clone.1 | convolution fusion | flops 173539328 | bytes 2916353 | tf_op jit(solution)/shard_map/while/body/eval_jaxpr/bts,brs->rbt/dot_general | solution.py:97
  139.8 3.9 %fusion.180 = f32[64,16,256]{2,0,1:T(8,128)} fusion(bf16[16,16,256]{2,1,0:T(8,128)(2,1)S(1)} %get-tuple-element.258, f32[16,256]{1,0:T(8,128)S(1)} %multiply_reduce_fusion.18, f32[16,256]{1,0:T(8,128)S(1)} %get-tuple-element.257, f32[64,16,256]{2,0,1:T(8,128)} %get-tuple-element.246, bf16[16,80,256]{2,1,0:T(8,128)(2,1)S(1)} %broadcast_select_fusion.7, ...), kind=kOutput, calls=%fused_computation.12.clone.1 | convolution fusion | flops 173539328 | bytes 2916353 | tf_op jit(solution)/shard_map/while/body/eval_jaxpr/bts,brs->rbt/dot_general | solution.py:97
  143.7 0.6 gather_fusion
  144.5 3.9 %fusion.180 = f32[64,16,256]{2,0,1:T(8,128)} fusion(bf16[16,16,256]{2,1,0:T(8,128)(2,1)S(1)} %get-tuple-element.258, f32[16,256]{1,0:T(8,128)S(1)} %multiply_reduce_fusion.18, f32[16,256]{1,0:T(8,128)S(1)} %get-tuple-element.257, f32[64,16,256]{2,0,1:T(8,128)} %get-tuple-element.246, bf16[16,80,256]{2,1,0:T(8,128)(2,1)S(1)} %broadcast_select_fusion.7, ...), kind=kOutput, calls=%fused_computation.12.clone.1 | convolution fusion | flops 173539328 | bytes 2916353 | tf_op jit(solution)/shard_map/while/body/eval_jaxpr/bts,brs->rbt/dot_general | solution.py:97
  148.4 1.3 copy.32
  149.8 4.0 %fusion.14 = f32[64,4096]{1,0:T(8,128)} fusion(f32[64,4096]{1,0:T(8,128)S(1)} %bitcast.112, bf16[64,512]{1,0:T(8,128)(2,1)S(1)} %copy-done.7, bf16[512,4096]{1,0:T(8,128)(2,1)} %get-tuple-element.158, f32[4096]{0:T(1024)S(1)} %get-tuple-element.157), kind=kOutput, calls=%fused_computation.30 | convolution fusion | flops 268959744 | bytes 6373376 | tf_op jit(solution)/shard_map/dot_general | solution.py:55
  (157 shorter events, 13.0 us)
Async XLA Ops:
  0.0 7.2 %copy-start = (bf16[16,4096]{1,0:T(8,128)(2,1)S(1)}, bf16[16,4096]{1,0:T(8,128)(2,1)}, u32[]{:S(2)}) copy-start(bf16[16,4096]{1,0:T(8,128)(2,1)} %param.9) | copy-start | bytes 393220
  0.0 7.3 %copy-start.2 = (s32[1,512]{1,0:T(1,128)S(1)}, s32[1,512]{1,0:T(1,128)}, u32[]{:S(2)}) copy-start(s32[1,512]{1,0:T(1,128)} %param.12) | copy-start | bytes 6148
  2.1 71.3 %collective-permute-start = (bf16[80,4096]{1,0:T(8,128)(2,1)S(1)}, bf16[80,4096]{1,0:T(8,128)(2,1)S(1)}, u32[]{:S(2)}, u32[]{:S(2)}) collective-permute-start(bf16[80,4096]{1,0:T(8,128)(2,1)S(1)} %constant_dynamic-update-slice_fusion), channel_id=1, source_target_pairs={{0,1},{1,2},{2,3},{3,4},{4,5},{5,6},{6,7},{7,8},{8,9},{9,10},{10,1... | collective-permute-start | bytes 1966088 | tf_op jit(solution)/shard_map/ppermute | solution.py:30
  4.5 68.8 %collective-permute-start.1 = (bf16[80,4096]{1,0:T(8,128)(2,1)S(1)}, bf16[80,4096]{1,0:T(8,128)(2,1)S(1)}, u32[]{:S(2)}, u32[]{:S(2)}) collective-permute-start(bf16[80,4096]{1,0:T(8,128)(2,1)S(1)} %constant_dynamic-update-slice_fusion), channel_id=1, source_target_pairs={{1,0},{2,1},{3,2},{4,3},{5,4},{6,5},{7,6},{8,7},{9,8},{10,9},{11,1... | collective-permute-start | bytes 1966088 | tf_op jit(solution)/shard_map/ppermute | solution.py:31
  8.8 4.6 %copy-start.1 = (bf16[64,4096]{1,0:T(8,128)(2,1)S(1)}, bf16[64,4096]{1,0:T(8,128)(2,1)}, u32[]{:S(2)}) copy-start(bf16[64,4096]{1,0:T(8,128)(2,1)} %param.10) | copy-start | bytes 1572868
  13.4 4.7 %copy-start.3 = (s32[1,4,512]{2,1,0:T(4,128)S(1)}, s32[1,4,512]{2,1,0:T(4,128)}, u32[]{:S(2)}) copy-start(s32[1,4,512]{2,1,0:T(4,128)} %param.13) | copy-start | bytes 24580
  14.8 9.5 %collective-permute-start.2 = (bf16[80,512]{1,0:T(8,128)(2,1)S(1)}, bf16[80,512]{1,0:T(8,128)(2,1)S(1)}, u32[]{:S(2)}, u32[]{:S(2)}) collective-permute-start(bf16[80,512]{1,0:T(8,128)(2,1)S(1)} %pad_maximum_fusion.1), channel_id=1, source_target_pairs={{0,1},{1,0},{2,3},{3,2},{4,5},{5,4},{6,7},{7,6},{8,9},{9,8},{10,11... | collective-permute-start | bytes 245768 | tf_op jit(solution)/shard_map/ppermute | solution.py:20
  18.2 5.9 %copy-start.4 = (s32[16,16]{1,0:T(8,128)S(1)}, s32[16,16]{1,0:T(8,128)}, u32[]{:S(2)}) copy-start(s32[16,16]{1,0:T(8,128)} %param.11) | copy-start | bytes 3076
  28.5 4.8 %collective-permute-start.3 = (bf16[80,512]{1,0:T(8,128)(2,1)S(1)}, bf16[80,512]{1,0:T(8,128)(2,1)S(1)}, u32[]{:S(2)}, u32[]{:S(2)}) collective-permute-start(bf16[80,512]{1,0:T(8,128)(2,1)S(1)} %pad_maximum_fusion.2), channel_id=1, source_target_pairs={{0,2},{2,0},{1,3},{3,1},{4,6},{6,4},{5,7},{7,5},{8,10},{10,8},{9,1... | collective-permute-start | bytes 245768 | tf_op jit(solution)/shard_map/ppermute | solution.py:20
  37.5 5.2 %collective-permute-start.4 = (bf16[80,512]{1,0:T(8,128)(2,1)S(1)}, bf16[80,512]{1,0:T(8,128)(2,1)S(1)}, u32[]{:S(2)}, u32[]{:S(2)}) collective-permute-start(bf16[80,512]{1,0:T(8,128)(2,1)S(1)} %pad_maximum_fusion.3), channel_id=1, source_target_pairs={{0,4},{4,0},{1,5},{5,1},{2,6},{6,2},{3,7},{7,3},{8,12},{12,8},{9,1... | collective-permute-start | bytes 245768 | tf_op jit(solution)/shard_map/ppermute | solution.py:20
  46.9 5.5 %collective-permute-start.5 = (bf16[80,512]{1,0:T(8,128)(2,1)S(1)}, bf16[80,512]{1,0:T(8,128)(2,1)S(1)}, u32[]{:S(2)}, u32[]{:S(2)}) collective-permute-start(bf16[80,512]{1,0:T(8,128)(2,1)S(1)} %pad_maximum_fusion.4), channel_id=1, source_target_pairs={{0,8},{8,0},{1,9},{9,1},{2,10},{10,2},{3,11},{11,3},{4,12},{12,4},... | collective-permute-start | bytes 245768 | tf_op jit(solution)/shard_map/ppermute | solution.py:20
  56.0 7.3 %collective-permute-start.6 = (bf16[80,512]{1,0:T(8,128)(2,1)S(1)}, bf16[80,512]{1,0:T(8,128)(2,1)S(1)}, u32[]{:S(2)}, u32[]{:S(2)}) collective-permute-start(bf16[80,512]{1,0:T(8,128)(2,1)S(1)} %pad_maximum_fusion.5), channel_id=1, source_target_pairs={{0,16},{16,0},{1,17},{17,1},{2,18},{18,2},{3,19},{19,3},{4,20},{20... | collective-permute-start | bytes 245768 | tf_op jit(solution)/shard_map/ppermute | solution.py:20
  64.1 4.6 %copy-start.6 = (bf16[512,512]{1,0:T(8,128)(2,1)S(1)}, bf16[512,512]{1,0:T(8,128)(2,1)}, u32[]{:S(2)}) copy-start(bf16[512,512]{1,0:T(8,128)(2,1)} %get-tuple-element.189) | copy-start | bytes 1572868
  66.6 5.3 %copy-start.5 = (bf16[512,512]{1,0:T(8,128)(2,1)S(1)}, bf16[512,512]{1,0:T(8,128)(2,1)}, u32[]{:S(2)}) copy-start(bf16[512,512]{1,0:T(8,128)(2,1)} %get-tuple-element.191) | copy-start | bytes 1572868
  148.4 1.4 copy-start.7
where the time goes:
time: 155 us; the launch traced here: 154 us
  matrix products  89.5 us (58%)
  local copies, waits for them, and re-layouts  23.5 us (15%)
  starting transfers between devices  19.5 us (13%)
  waiting for transfers between devices  10.3 us (7%)
  other arithmetic  9.9 us (6%)
    dot_general x16, matrix products, one_turn(): jnp.einsum('bts,brs->rbt', weights, source[:, DIM:], preferred_element_ty...  60.6 us
    ppermute x5, starting transfers between devices, partner(): return lax.ppermute(block, axis, route)  15.8 us
    dot_general x9, matrix products, kernel_block(): jnp.einsum('dm,dn->mn', left, right, preferred_element_type=jnp.float32)  11.8 us
    ppermute x5, waiting for transfers between devices, partner(): return lax.ppermute(block, axis, route)  10.3 us
    gather x16, local copies, waits for them, and re-layouts, one_turn(): source = jnp.take(leaves, leaf_ids[:, turn], axis=0)  9.43 us
    dot_general x5, matrix products, carry_values(): jnp.dot(values, block, preferred_element_type=jnp.float32) / totals[None, :]  8.02 us
    reduce_sum x1, other arithmetic, carry_values(): totals = jnp.sum(block.astype(jnp.float32), 0)  5.88 us
    gather x8, local copies, waits for them, and re-layouts, parent_node(): parent_x = jnp.take(joined_x, chosen, axis=1)  5.85 us
  transfers between devices with their start and end apart: 7, of which 4 were waited for; matrix products, arithmetic and copies ran while one was open for 27% of the time, Pallas kernels for 0%

commit v1 on v0

v1 whole, which is shorter than its diff:
```python
import functools

import jax
import jax.numpy as jnp
from jax import lax
from jax.experimental import pallas as pl
from jax.experimental.pallas import tpu as pltpu
from jax.sharding import PartitionSpec as P

DIM = 16
NRHS = 64
DEPTH = 64
GAMMA = 0.125
LOG2E = 1.4426950408889634
MESH = pl.DeviceIdType.MESH
F32 = jnp.float32
BF16 = jnp.bfloat16


def split3(value):
    high = value.astype(BF16).astype(F32)
    rest = value - high
    middle = rest.astype(BF16).astype(F32)
    return [high, middle, rest - middle]


def norms(x32):
    return split3(-(GAMMA * LOG2E) * jnp.sum(x32 * x32, 0, keepdims=True))


def padding(x32):
    return [jnp.zeros((DEPTH - 3 * DIM - 6, x32.shape[1]), F32)]


def row_side(x):
    x32 = x.astype(F32)
    ones = jnp.ones((1, x32.shape[1]), F32)
    parts = split3((2.0 * GAMMA * LOG2E) * x32) + norms(x32) + [ones] * 3 + padding(x32)
    return jnp.concatenate(parts, 0).T.astype(BF16)


def column_side(x):
    x32 = x.astype(F32)
    ones = jnp.ones((1, x32.shape[1]), F32)
    parts = [x32] * 3 + [ones] * 3 + norms(x32) + padding(x32)
    return jnp.concatenate(parts, 0).astype(BF16)


def dot(left, right):
    return jnp.dot(left, right, preferred_element_type=F32)


def dot_nt(left, right):
    return lax.dot_general(left, right, (((1,), (1,)), ((), ())), preferred_element_type=F32)


def gaussian(rows, columns):
    return jnp.exp2(dot(rows, columns)).astype(BF16)


def column_sums(block):
    return jnp.sum(block.astype(F32), 0, keepdims=True)


def picked(source, chosen, first):
    index = lax.broadcasted_iota(jnp.int32, (source.shape[1], chosen.shape[1]), 0) + first
    return dot(source, jnp.where(index == chosen, 1.0, 0.0).astype(BF16))


def kernel(
    inner_levels, outer_levels, near_ref, x_ref, q_ref, device_ref, tree_ref, out_ref,
    xhalo, qhalo, qall, rows, cols, block0, total0, acc, nodes, sibs, blocks, totals, beside,
    halo_send, halo_recv, tree_send, tree_recv,
):
    inner = 1 << inner_levels
    levels = inner_levels + outer_levels
    outer_id, inner_id = lax.axis_index("outer"), lax.axis_index("inner")
    count = inner << outer_levels
    position = outer_id * inner + inner_id
    n = x_ref.shape[1]
    leaf_dev, n_near = near_ref.shape
    leaf = n // leaf_dev
    size = device_ref.shape[1]
    has_left, has_right = position > 0, position < count - 1
    left, right = jnp.maximum(position - 1, 0), jnp.minimum(position + 1, count - 1)
    left_id = (left // inner, left % inner)
    right_id = (right // inner, right % inner)

    bits, partners = [], []
    for k in range(levels):
        if k < inner_levels:
            bit = (inner_id // (1 << k)) % 2
            partners.append((outer_id, inner_id + (1 - 2 * bit) * (1 << k)))
        else:
            step = 1 << (k - inner_levels)
            bit = (outer_id // step) % 2
            partners.append((outer_id + (1 - 2 * bit) * step, inner_id))
        bits.append(bit)

    barrier = pltpu.get_barrier_semaphore()
    for peer in partners:
        pl.semaphore_signal(barrier, inc=1, device_id=peer, device_id_type=MESH)

    @pl.when(has_left)
    def _():
        pl.semaphore_signal(barrier, inc=1, device_id=left_id, device_id_type=MESH)

    @pl.when(has_right)
    def _():
        pl.semaphore_signal(barrier, inc=1, device_id=right_id, device_id_type=MESH)

    chunk = 512
    wide = n // chunk

    def pick(c, total):
        part = pl.ds(pl.multiple_of(c * chunk, chunk), chunk)
        cols[:, part] = column_side(x_ref[:, part])
        return total + picked(x_ref[:, part], device_ref[...], c * chunk)

    base_x = lax.fori_loop(0, wide, pick, jnp.zeros((DIM, size), F32)).astype(BF16)

    sides = (position + count - 1) // count + 1 - (position + 1) // count
    pl.semaphore_wait(barrier, levels + sides)

    def halo(source, target, which, peer):
        return pltpu.make_async_remote_copy(
            src_ref=source, dst_ref=target, send_sem=halo_send.at[which],
            recv_sem=halo_recv.at[which], device_id=peer, device_id_type=MESH,
        )

    rightward = [
        halo(x_ref, xhalo.at[0], 0, right_id),
        halo(q_ref, qhalo.at[0], 1, right_id),
    ]
    leftward = [
        halo(x_ref, xhalo.at[1], 2, left_id),
        halo(q_ref, qhalo.at[1], 3, left_id),
    ]

    @pl.when(has_right)
    def _():
        for copy in rightward:
            copy.start()

    @pl.when(has_left)
    def _():
        for copy in leftward:
            copy.start()

    nodes[0, :DIM, :] = base_x
    base_rows = row_side(base_x)
    acc[...] = jnp.zeros_like(acc)

    def base(c, _):
        part = pl.ds(pl.multiple_of(c * chunk, chunk), chunk)
        block = gaussian(base_rows, cols[:, part])
        total = column_sums(block)
        block0[:, part] = block
        total0[:, part] = 1.0 / total
        weights = (q_ref[:, part].astype(F32) / total).astype(BF16)
        acc[...] += dot_nt(weights, block)
        return 0

    lax.fori_loop(0, wide, base, 0)
    nodes[0, DIM:, :] = acc[...].astype(BF16)

    exchanges = [
        pltpu.make_async_remote_copy(
            src_ref=nodes.at[k], dst_ref=sibs.at[k], send_sem=tree_send.at[k],
            recv_sem=tree_recv.at[k], device_id=partners[k], device_id_type=MESH,
        )
        for k in range(levels)
    ]
    exchanges[0].start()

    def prepare(first, x_source, q_source):
        def one(j, _):
            part = pl.ds(pl.multiple_of(j * leaf, leaf), leaf)
            rows[first + j] = row_side(x_source[:, part])
            qall[first + j] = q_source[:, part]
            return 0

        lax.fori_loop(0, leaf_dev, one, 0)

    def near(b, _):
        part = pl.ds(pl.multiple_of(b * leaf, leaf), leaf)
        columns = cols[:, part]
        weights, loads = [], []
        for turn in range(n_near):
            number = near_ref[b, turn] - (position - 1) * leaf_dev
            number = jnp.minimum(jnp.maximum(number, 0), 3 * leaf_dev - 1)
            weights.append(gaussian(rows[number], columns))
            loads.append(qall[number])
        out_ref[:, part] = dot(jnp.concatenate(loads, 1), jnp.concatenate(weights, 0))
        return 0

    def climb(k):
        own, sib = nodes[k], sibs[k]
        joined_x = jnp.concatenate([own[:DIM], sib[:DIM]], 1)
        shifted = tree_ref[0, k : k + 1, :] + bits[k] * size
        chosen = jnp.where(shifted >= 2 * size, shifted - 2 * size, shifted)
        parent_x = picked(joined_x, chosen, 0).astype(BF16)
        parent_rows = row_side(parent_x)
        up = jnp.zeros((NRHS, size), F32)
        for half in (own, sib):
            block = gaussian(parent_rows, column_side(half[:DIM]))
            total = column_sums(block)
            if half is own:
                blocks[k] = block
                totals[k : k + 1, :] = total
            up = up + dot_nt((half[DIM:].astype(F32) / total).astype(BF16), block)
        nodes[k + 1, :DIM, :] = parent_x
        nodes[k + 1, DIM:, :] = up.astype(BF16)
        exchanges[k + 1].start()

    def across(k):
        own, sib = nodes[k], sibs[k]
        beside[k] = dot(sib[DIM:], gaussian(row_side(sib[:DIM]), column_side(own[:DIM])))

    prepare(leaf_dev, x_ref, q_ref)
    share = max(1, min(2, leaf_dev // levels))
    done = 0
    for k in range(levels):
        exchanges[k].wait_recv()
        if k < levels - 1:
            climb(k)
        across(k)
        if k == 0:
            @pl.when(has_left)
            def _():
                for copy in rightward:
                    copy.wait_recv()

            prepare(0, xhalo.at[0], qhalo.at[0])

            @pl.when(has_right)
            def _():
                for copy in leftward:
                    copy.wait_recv()

            prepare(2 * leaf_dev, xhalo.at[1], qhalo.at[1])
        ahead = min(leaf_dev, done + share) if k < levels - 1 else leaf_dev
        if ahead > done:
            lax.fori_loop(done, ahead, near, 0)
        done = ahead

    down = beside[levels - 1].astype(BF16)
    for k in range(levels - 2, -1, -1):
        down = (beside[k] + dot(down, blocks[k]) / totals[k : k + 1, :]).astype(BF16)

    def far(c, _):
        part = pl.ds(pl.multiple_of(c * chunk, chunk), chunk)
        out_ref[:, part] += dot(down, block0[:, part]) * total0[:, part]
        return 0

    lax.fori_loop(0, wide, far, 0)

    for copy in exchanges:
        copy.wait_send()

    @pl.when(has_right)
    def _():
        for copy in rightward:
            copy.wait_send()

    @pl.when(has_left)
    def _():
        for copy in leftward:
            copy.wait_send()


def body(points, charges, near_leaves, skel_device, skel_tree):
    inner_levels = lax.axis_size("inner").bit_length() - 1
    outer_levels = lax.axis_size("outer").bit_length() - 1
    levels = inner_levels + outer_levels
    n, size = points.shape[1], skel_device.shape[1]
    leaf_dev = near_leaves.shape[0]
    leaf = n // leaf_dev
    vmem = pl.BlockSpec(memory_space=pltpu.VMEM)
    node = (levels, DIM + NRHS, size)
    return pl.pallas_call(
        functools.partial(kernel, inner_levels, outer_levels),
        out_shape=jax.ShapeDtypeStruct((NRHS, n), F32),
        in_specs=[pl.BlockSpec(memory_space=pltpu.SMEM)] + [vmem] * 4,
        out_specs=vmem,
        scratch_shapes=[
            pltpu.VMEM((2, DIM, n), BF16),
            pltpu.VMEM((2, NRHS, n), BF16),
            pltpu.VMEM((3 * leaf_dev, NRHS, leaf), BF16),
            pltpu.VMEM((3 * leaf_dev, leaf, DEPTH), BF16),
            pltpu.VMEM((DEPTH, n), BF16),
            pltpu.VMEM((size, n), BF16),
            pltpu.VMEM((1, n), F32),
            pltpu.VMEM((NRHS, size), F32),
            pltpu.VMEM(node, BF16),
            pltpu.VMEM(node, BF16),
            pltpu.VMEM((levels, size, size), BF16),
            pltpu.VMEM((levels, size), F32),
            pltpu.VMEM((levels, NRHS, size), F32),
            pltpu.SemaphoreType.DMA((4,)),
            pltpu.SemaphoreType.DMA((4,)),
            pltpu.SemaphoreType.DMA((levels,)),
            pltpu.SemaphoreType.DMA((levels,)),
        ],
        compiler_params=pltpu.CompilerParams(
            collective_id=0, has_side_effects=True, vmem_limit_bytes=50 << 20
        ),
        name="skeleton_matvec",
    )(near_leaves, points, charges, skel_device, skel_tree)


def solution(mesh):
    return jax.shard_map(
        body,
        mesh=mesh,
        in_specs=(
            P(None, ("outer", "inner")),
            P(None, ("outer", "inner")),
            P(("outer", "inner"), None),
            P(("outer", "inner"), None),
            P(("outer", "inner"), None, None),
        ),
        out_specs=P(None, ("outer", "inner")),
        check_vma=False,
    )
```

time: 155 us -> 58.5 us (0.38)
  the two profiles are of different devices: /device:TPU:0 before, /device:TPU:6 now
where the time goes in v1:
time: 58.5 us; the launch traced here: 58.2 us
  Pallas kernels  53.2 us (91%)
  local copies, waits for them, and re-layouts  4.99 us (9%)
    pallas_call x1, Pallas kernels, body(): pl.pallas_call(functools.partial(kernel, inner_levels, outer_levels), out...  53.2 us
    unnamed x11, local copies, waits for them, and re-layouts  4.99 us

profile of v1, /device:TPU:6, one launch (start us, length us, event | category | flops | bytes accessed | tf_op | source)
XLA Modules:
  0.0 58.2 jit_solution(3602726535398127374)
XLA Ops:
  0.0 0.0 copy-start
  0.0 1.0 %copy-done = bf16[64,4096]{1,0:T(8,128)(2,1)S(1)} copy-done((bf16[64,4096]{1,0:T(8,128)(2,1)S(1)}, bf16[64,4096]{1,0:T(8,128)(2,1)}, u32[]{:S(2)}) %copy-start) | copy-done | bytes 524312
  1.0 0.0 copy-start.1
  1.0 0.9 %copy-done.1 = bf16[16,4096]{1,0:T(8,128)(2,1)S(1)} copy-done((bf16[16,4096]{1,0:T(8,128)(2,1)S(1)}, bf16[16,4096]{1,0:T(8,128)(2,1)}, u32[]{:S(2)}) %copy-start.1) | copy-done | bytes 131096
  1.9 0.0 copy-start.2
  1.9 0.7 %copy-done.2 = s32[16,16]{1,0:T(8,128)S(1)} copy-done((s32[16,16]{1,0:T(8,128)S(1)}, s32[16,16]{1,0:T(8,128)}, u32[]{:S(2)}) %copy-start.2) | copy-done | bytes 1048
  2.6 0.0 copy-start.3
  2.6 0.7 %copy-done.3 = s32[1,4,512]{2,1,0:T(4,128)S(1)} copy-done((s32[1,4,512]{2,1,0:T(4,128)S(1)}, s32[1,4,512]{2,1,0:T(4,128)}, u32[]{:S(2)}) %copy-start.3) | copy-done | bytes 8216
  3.3 0.0 copy-start.4
  3.3 0.7 %copy-done.4 = s32[1,512]{1,0:T(1,128)S(1)} copy-done((s32[1,512]{1,0:T(1,128)S(1)}, s32[1,512]{1,0:T(1,128)}, u32[]{:S(2)}) %copy-start.4) | copy-done | bytes 2072
  4.0 53.2 %skeleton_matvec.1 = f32[64,4096]{1,0:T(8,128)S(1)} custom-call(s32[16,16]{1,0:T(8,128)S(1)} %copy-done.2, bf16[16,4096]{1,0:T(8,128)(2,1)S(1)} %copy-done.1, bf16[64,4096]{1,0:T(8,128)(2,1)S(1)} %copy-done, s32[1,512]{1,0:T(1,128)S(1)} %copy-done.4, s32[1,4,512]{2,1,0:T(4,128)S(1)} %copy-done.3), custom_call_target="tpu_custom_call" | custom-call | tf_op jit(solution)/shard_map/skeleton_matvec/pallas_call | solution.py:281
  57.2 1.0 %copy.7 = f32[64,4096]{1,0:T(8,128)} copy(f32[64,4096]{1,0:T(8,128)S(1)} %skeleton_matvec.1) | data formatting | bytes 2097152
Async XLA Ops:
  0.0 1.0 %copy-start = (bf16[64,4096]{1,0:T(8,128)(2,1)S(1)}, bf16[64,4096]{1,0:T(8,128)(2,1)}, u32[]{:S(2)}) copy-start(bf16[64,4096]{1,0:T(8,128)(2,1)} %q_ref.1) | copy-start | bytes 1572868
  1.0 0.9 %copy-start.1 = (bf16[16,4096]{1,0:T(8,128)(2,1)S(1)}, bf16[16,4096]{1,0:T(8,128)(2,1)}, u32[]{:S(2)}) copy-start(bf16[16,4096]{1,0:T(8,128)(2,1)} %x_ref.1) | copy-start | bytes 393220
  1.9 0.7 %copy-start.2 = (s32[16,16]{1,0:T(8,128)S(1)}, s32[16,16]{1,0:T(8,128)}, u32[]{:S(2)}) copy-start(s32[16,16]{1,0:T(8,128)} %near_ref.1) | copy-start | bytes 3076
  2.6 0.7 %copy-start.3 = (s32[1,4,512]{2,1,0:T(4,128)S(1)}, s32[1,4,512]{2,1,0:T(4,128)}, u32[]{:S(2)}) copy-start(s32[1,4,512]{2,1,0:T(4,128)} %tree_ref.1) | copy-start | bytes 24580
  3.3 0.7 %copy-start.4 = (s32[1,512]{1,0:T(1,128)S(1)}, s32[1,512]{1,0:T(1,128)}, u32[]{:S(2)}) copy-start(s32[1,512]{1,0:T(1,128)} %device_ref.1) | copy-start | bytes 6148

commit v2 on v1

--- a/solution.py
+++ b/solution.py
@@ -68,9 +68,9 @@
 
 
 def kernel(
-    inner_levels, outer_levels, near_ref, x_ref, q_ref, device_ref, tree_ref, out_ref,
-    xhalo, qhalo, qall, rows, cols, block0, total0, acc, nodes, sibs, blocks, totals, beside,
-    halo_send, halo_recv, tree_send, tree_recv,
+    inner_levels, outer_levels, near_hbm, x_hbm, q_hbm, device_hbm, tree_hbm, out_ref,
+    near_ref, x_ref, q_ref, device_ref, tree_ref, xhalo, qhalo, qall, rows, cols, block0, total0, acc, nodes, sibs, blocks, totals, beside,
+    halo_send, halo_recv, tree_send, tree_recv, local_sem,
 ):
     inner = 1 << inner_levels
     levels = inner_levels + outer_levels
@@ -97,6 +97,15 @@
             partners.append((outer_id + (1 - 2 * bit) * step, inner_id))
         bits.append(bit)
 
+    sources = (x_hbm, device_hbm, q_hbm, tree_hbm, near_hbm)
+    targets = (x_ref, device_ref, q_ref, tree_ref, near_ref)
+    loads = [
+        pltpu.make_async_copy(source, target, local_sem.at[i])
+        for i, (source, target) in enumerate(zip(sources, targets))
+    ]
+    for load in loads:
+        load.start()
+
     barrier = pltpu.get_barrier_semaphore()
     for peer in partners:
         pl.semaphore_signal(barrier, inc=1, device_id=peer, device_id_type=MESH)
@@ -117,10 +126,12 @@
         cols[:, part] = column_side(x_ref[:, part])
         return total + picked(x_ref[:, part], device_ref[...], c * chunk)
 
-    base_x = lax.fori_loop(0, wide, pick, jnp.zeros((DIM, size), F32)).astype(BF16)
-
-    sides = (position + count - 1) // count + 1 - (position + 1) // count
-    pl.semaphore_wait(barrier, levels + sides)
+    loads[0].wait()
+    loads[1].wait()
+    base_x = lax.fori_loop(0, wide, pick, jnp.zeros((DIM, size), F32), unroll=4).astype(BF16)
+
+    beside_us = (position + count - 1) // count + 1 - (position + 1) // count
+    pl.semaphore_wait(barrier, levels + beside_us)
 
     def halo(source, target, which, peer):
         return pltpu.make_async_remote_copy(
@@ -129,12 +140,12 @@
         )
 
     rightward = [
-        halo(x_ref, xhalo.at[0], 0, right_id),
-        halo(q_ref, qhalo.at[0], 1, right_id),
+        halo(x_hbm, xhalo.at[0], 0, right_id),
+        halo(q_hbm, qhalo.at[0], 1, right_id),
     ]
     leftward = [
-        halo(x_ref, xhalo.at[1], 2, left_id),
-        halo(q_ref, qhalo.at[1], 3, left_id),
+        halo(x_hbm, xhalo.at[1], 2, left_id),
+        halo(q_hbm, qhalo.at[1], 3, left_id),
     ]
 
     @pl.when(has_right)
@@ -156,12 +167,15 @@
         block = gaussian(base_rows, cols[:, part])
         total = column_sums(block)
         block0[:, part] = block
-        total0[:, part] = 1.0 / total
-        weights = (q_ref[:, part].astype(F32) / total).astype(BF16)
+        inverse = 1.0 / total
+        total0[:, part] = inverse
+        weights = (q_ref[:, part].astype(F32) * inverse).astype(BF16)
         acc[...] += dot_nt(weights, block)
         return 0
 
-    lax.fori_loop(0, wide, base, 0)
+    for load in loads[2:]:
+        load.wait()
+    lax.fori_loop(0, wide, base, 0, unroll=2)
     nodes[0, DIM:, :] = acc[...].astype(BF16)
 
     exchanges = [
@@ -180,18 +194,18 @@
             qall[first + j] = q_source[:, part]
             return 0
 
-        lax.fori_loop(0, leaf_dev, one, 0)
+        lax.fori_loop(0, leaf_dev, one, 0, unroll=8)
 
     def near(b, _):
         part = pl.ds(pl.multiple_of(b * leaf, leaf), leaf)
         columns = cols[:, part]
-        weights, loads = [], []
+        weights, sides = [], []
         for turn in range(n_near):
             number = near_ref[b, turn] - (position - 1) * leaf_dev
             number = jnp.minimum(jnp.maximum(number, 0), 3 * leaf_dev - 1)
             weights.append(gaussian(rows[number], columns))
-            loads.append(qall[number])
-        out_ref[:, part] = dot(jnp.concatenate(loads, 1), jnp.concatenate(weights, 0))
+            sides.append(qall[number])
+        out_ref[:, part] = dot(jnp.concatenate(sides, 1), jnp.concatenate(weights, 0))
         return 0
 
     def climb(k):
@@ -204,11 +218,11 @@
         up = jnp.zeros((NRHS, size), F32)
         for half in (own, sib):
             block = gaussian(parent_rows, column_side(half[:DIM]))
-            total = column_sums(block)
+            inverse = 1.0 / column_sums(block)
             if half is own:
                 blocks[k] = block
-                totals[k : k + 1, :] = total
-            up = up + dot_nt((half[DIM:].astype(F32) / total).astype(BF16), block)
+                totals[k : k + 1, :] = inverse
+            up = up + dot_nt((half[DIM:].astype(F32) * inverse).astype(BF16), block)
         nodes[k + 1, :DIM, :] = parent_x
         nodes[k + 1, DIM:, :] = up.astype(BF16)
         exchanges[k + 1].start()
@@ -226,6 +240,7 @@
             climb(k)
         across(k)
         if k == 0:
+
             @pl.when(has_left)
             def _():
                 for copy in rightward:
@@ -246,14 +261,14 @@
 
     down = beside[levels - 1].astype(BF16)
     for k in range(levels - 2, -1, -1):
-        down = (beside[k] + dot(down, blocks[k]) / totals[k : k + 1, :]).astype(BF16)
+        down = (beside[k] + dot(down, blocks[k]) * totals[k : k + 1, :]).astype(BF16)
 
     def far(c, _):
         part = pl.ds(pl.multiple_of(c * chunk, chunk), chunk)
         out_ref[:, part] += dot(down, block0[:, part]) * total0[:, part]
         return 0
 
-    lax.fori_loop(0, wide, far, 0)
+    lax.fori_loop(0, wide, far, 0, unroll=2)
 
     for copy in exchanges:
         copy.wait_send()
@@ -281,9 +296,14 @@
     return pl.pallas_call(
         functools.partial(kernel, inner_levels, outer_levels),
         out_shape=jax.ShapeDtypeStruct((NRHS, n), F32),
-        in_specs=[pl.BlockSpec(memory_space=pltpu.SMEM)] + [vmem] * 4,
+        in_specs=[pl.BlockSpec(memory_space=pltpu.HBM)] * 5,
         out_specs=vmem,
         scratch_shapes=[
+            pltpu.SMEM(near_leaves.shape, jnp.int32),
+            pltpu.VMEM(points.shape, BF16),
+            pltpu.VMEM(charges.shape, BF16),
+            pltpu.VMEM(skel_device.shape, jnp.int32),
+            pltpu.VMEM(skel_tree.shape, jnp.int32),
             pltpu.VMEM((2, DIM, n), BF16),
             pltpu.VMEM((2, NRHS, n), BF16),
             pltpu.VMEM((3 * leaf_dev, NRHS, leaf), BF16),
@@ -301,6 +321,7 @@
             pltpu.SemaphoreType.DMA((4,)),
             pltpu.SemaphoreType.DMA((levels,)),
             pltpu.SemaphoreType.DMA((levels,)),
+            pltpu.SemaphoreType.DMA((5,)),
         ],
         compiler_params=pltpu.CompilerParams(
             collective_id=0, has_side_effects=True, vmem_limit_bytes=50 << 20

time: 58.5 us -> 57.6 us (0.985)
  the two profiles are of different devices: /device:TPU:6 before, /device:TPU:0 now
where the time goes in v2:
time: 57.6 us; the launch traced here: 57.3 us
  Pallas kernels  52.3 us (91%)
  local copies, waits for them, and re-layouts  4.99 us (9%)
    pallas_call x1, Pallas kernels, body(): pl.pallas_call(functools.partial(kernel, inner_levels, outer_levels), out...  52.3 us
    unnamed x11, local copies, waits for them, and re-layouts  4.99 us

profile of v2, /device:TPU:0, one launch (start us, length us, event | category | flops | bytes accessed | tf_op | source)
XLA Modules:
  0.0 57.3 jit_solution(16368126956537082250)
XLA Ops:
  0.0 0.0 copy-start
  0.0 1.0 %copy-done = bf16[64,4096]{1,0:T(8,128)(2,1)S(1)} copy-done((bf16[64,4096]{1,0:T(8,128)(2,1)S(1)}, bf16[64,4096]{1,0:T(8,128)(2,1)}, u32[]{:S(2)}) %copy-start) | copy-done | bytes 524312
  1.0 0.0 copy-start.1
  1.0 0.9 %copy-done.1 = bf16[16,4096]{1,0:T(8,128)(2,1)S(1)} copy-done((bf16[16,4096]{1,0:T(8,128)(2,1)S(1)}, bf16[16,4096]{1,0:T(8,128)(2,1)}, u32[]{:S(2)}) %copy-start.1) | copy-done | bytes 131096
  1.9 0.0 copy-start.2
  1.9 0.7 %copy-done.2 = s32[16,16]{1,0:T(8,128)S(1)} copy-done((s32[16,16]{1,0:T(8,128)S(1)}, s32[16,16]{1,0:T(8,128)}, u32[]{:S(2)}) %copy-start.2) | copy-done | bytes 1048
  2.6 0.0 copy-start.3
  2.6 0.7 %copy-done.3 = s32[1,4,512]{2,1,0:T(4,128)S(1)} copy-done((s32[1,4,512]{2,1,0:T(4,128)S(1)}, s32[1,4,512]{2,1,0:T(4,128)}, u32[]{:S(2)}) %copy-start.3) | copy-done | bytes 8216
  3.3 0.0 copy-start.4
  3.3 0.7 %copy-done.4 = s32[1,512]{1,0:T(1,128)S(1)} copy-done((s32[1,512]{1,0:T(1,128)S(1)}, s32[1,512]{1,0:T(1,128)}, u32[]{:S(2)}) %copy-start.4) | copy-done | bytes 2072
  4.0 52.3 %skeleton_matvec.1 = f32[64,4096]{1,0:T(8,128)S(1)} custom-call(s32[16,16]{1,0:T(8,128)S(1)} %copy-done.2, bf16[16,4096]{1,0:T(8,128)(2,1)S(1)} %copy-done.1, bf16[64,4096]{1,0:T(8,128)(2,1)S(1)} %copy-done, s32[1,512]{1,0:T(1,128)S(1)} %copy-done.4, s32[1,4,512]{2,1,0:T(4,128)S(1)} %copy-done.3), custom_call_target="tpu_custom_call" | custom-call | tf_op jit(solution)/shard_map/skeleton_matvec/pallas_call | solution.py:296
  56.3 1.0 %copy.7 = f32[64,4096]{1,0:T(8,128)} copy(f32[64,4096]{1,0:T(8,128)S(1)} %skeleton_matvec.1) | data formatting | bytes 2097152
Async XLA Ops:
  0.0 1.0 %copy-start = (bf16[64,4096]{1,0:T(8,128)(2,1)S(1)}, bf16[64,4096]{1,0:T(8,128)(2,1)}, u32[]{:S(2)}) copy-start(bf16[64,4096]{1,0:T(8,128)(2,1)} %q_hbm.1) | copy-start | bytes 1572868
  1.0 0.9 %copy-start.1 = (bf16[16,4096]{1,0:T(8,128)(2,1)S(1)}, bf16[16,4096]{1,0:T(8,128)(2,1)}, u32[]{:S(2)}) copy-start(bf16[16,4096]{1,0:T(8,128)(2,1)} %x_hbm.1) | copy-start | bytes 393220
  1.9 0.7 %copy-start.2 = (s32[16,16]{1,0:T(8,128)S(1)}, s32[16,16]{1,0:T(8,128)}, u32[]{:S(2)}) copy-start(s32[16,16]{1,0:T(8,128)} %near_hbm.1) | copy-start | bytes 3076
  2.6 0.7 %copy-start.3 = (s32[1,4,512]{2,1,0:T(4,128)S(1)}, s32[1,4,512]{2,1,0:T(4,128)}, u32[]{:S(2)}) copy-start(s32[1,4,512]{2,1,0:T(4,128)} %tree_hbm.1) | copy-start | bytes 24580
  3.3 0.7 %copy-start.4 = (s32[1,512]{1,0:T(1,128)S(1)}, s32[1,512]{1,0:T(1,128)}, u32[]{:S(2)}) copy-start(s32[1,512]{1,0:T(1,128)} %device_hbm.1) | copy-start | bytes 6148
